TPU v7x, 32 devices: a whole 2x2x4 slice. The times are simulated.
32 devices in a mesh: tile: 8 (over z, x), slab: 4 (over y, core).
Axes of the slice: x: 2, y: 2, z: 4, core: 2. Of those that a mesh axis runs over, the one named last changes fastest.
Arguments:
- object_field: bfloat16 [2, 8, 1024, 512], P(None, 'slab', 'tile')
- probe_wave: bfloat16 [2, 128, 128], replicated, may hold values from -6 to 6
- prop_phase: float32 [128, 128], replicated, may hold values from -3.140625 to 3.140625
- intensity: float32 [16, 128, 128], P('tile'), may hold values from 0 to 4
- patch_rows: int32 [16], replicated, may hold values from 0 to 127
- patch_cols: int32 [16], replicated, may hold values from 0 to 384
Outputs:
- grad_object: bfloat16 [2, 8, 1024, 512], P(None, 'slab', 'tile')
Inputs may be any that keep to these rules, and one draw needn't show every extreme that they name: `patch_rows`: a window of tile t covers rows of tile t and of the next tile (the first tile after the last).
All inputs are finite; a program needn't handle non-finite values.
Results may differ from a plain program's by a relative error of at most 0.005.
Values may be sent and summed in bfloat16 or wider, within the bound.
A program may use at most 64 MiB of HBM per device.

v0:
```python
import functools
import math

import jax
import jax.numpy as jnp
import numpy as np
from jax import lax
from jax.experimental import pallas as pl
from jax.experimental.pallas import tpu as pltpu
from jax.sharding import PartitionSpec as P

F32 = jnp.float32
BF16 = jnp.bfloat16


def fourier_parts(window):
    index = np.arange(window)
    angle = (index[:, None] * index[None, :] % window) * (-2.0 * math.pi / window)
    real = np.cos(angle) / math.sqrt(window)
    imag = np.sin(angle) / math.sqrt(window)
    big = np.block([[real, imag], [-imag, real]]).astype(np.float32)
    high = big.astype(BF16)
    low = (big - high.astype(np.float32)).astype(BF16)
    return np.concatenate([high, high, low], axis=0)


def split(value):
    high = value.astype(BF16)
    return high, (value - high.astype(F32)).astype(BF16)


def from_right(field, right, window):
    high, low = split(jnp.concatenate(field, axis=1))
    product = jnp.dot(
        jnp.concatenate([high, low, high], axis=1), right[...], preferred_element_type=F32
    )
    return product[:, :window], product[:, window:]


def transform(field, right, window):
    first = [from_right(f, right, window) for f in field]
    return [from_right((re.T, im.T), right, window) for re, im in first]


def times(a, b):
    return a[0] * b[0] - a[1] * b[1], a[0] * b[1] + a[1] * b[0]


def conj_times(a, b):
    return a[0] * b[0] + a[1] * b[1], a[0] * b[1] - a[1] * b[0]


def conj(a):
    return a[0], -a[1]


def load(ref, lead, count, window):
    out = []
    for p in range(count):
        block = ref[lead, p].astype(F32)
        out.append((block[:, :window], block[:, window:]))
    return out


def store(ref, lead, field):
    for p, (re, im) in enumerate(field):
        ref[lead, p] = jnp.concatenate([re, im], axis=1).astype(ref.dtype)


MESH = pl.DeviceIdType.MESH


def one_hot(shape, along, offset):
    here = lax.broadcasted_iota(jnp.int32, shape, along)
    there = lax.broadcasted_iota(jnp.int32, shape, 1 - along)
    return jnp.where(here == there + offset, 1.0, 0.0).astype(BF16)


def halves(block, window):
    return block[:, :window], block[:, window:]


def kernel(
    tiles, sections, row_ref, col_ref, obj, probe, phase, measured, right_in, out,
    cut_prior, cut_own, low, patches, psi, work, terms, spill, spilled, right, turned,
    tile_send, tile_recv, cross_send, cross_recv, pair_send, pair_recv, back_send, back_recv, table_sem, go,
):
    layers, window, columns = obj.shape[1], obj.shape[2], obj.shape[3]
    count, slices = measured.shape[0], patches.shape[0]
    groups = sections // 2
    last = slices - 1
    tile = lax.axis_index("tile")
    slab = lax.axis_index("slab")
    after, prior = lax.rem(tile + 1, tiles), lax.rem(tile + tiles - 1, tiles)
    group, side = slab // 2, lax.rem(slab, 2)
    partner = slab + 1 - 2 * side
    first_own = slab * layers

    def remote(src, dst, send, recv, **device):
        return pltpu.make_async_remote_copy(
            src_ref=src, dst_ref=dst, send_sem=send, recv_sem=recv,
            device_id=device, device_id_type=MESH,
        )

    table = pltpu.make_async_copy(right_in, right, table_sem)
    table.start()
    barrier = pltpu.get_barrier_semaphore()
    greeted = [{"tile": after}, {"tile": prior}, {"slab": partner}]
    for step in range(1, groups):
        greeted.append({"slab": lax.rem(group + step, groups) * 2 + side})
    for device in greeted:
        pl.semaphore_signal(barrier, inc=1, device_id=device, device_id_type=MESH)

    def columns_of(base):
        return [col_ref[base * count + p] for p in range(count)]

    prior_cols, own_cols = columns_of(prior), columns_of(tile)
    own_rows = [row_ref[tile * count + p] for p in range(count)]

    def cut(cols, layer, target):
        pick = jnp.concatenate([one_hot((columns, window), 0, c) for c in cols], axis=1)
        both = jnp.concatenate([obj[0, layer], obj[1, layer]], axis=0)
        got = jnp.dot(both, pick, preferred_element_type=F32).astype(BF16)
        for p in range(count):
            part = got[:, p * window : (p + 1) * window]
            target[layer, p] = jnp.concatenate([part[:window], part[window:]], axis=1)

    def tile_copy(layer):
        return remote(
            cut_prior.at[layer], low.at[layer], tile_send.at[layer], tile_recv.at[layer], tile=prior
        )

    for layer in range(layers):
        cut(prior_cols, layer, cut_prior)
    pl.semaphore_wait(barrier, len(greeted))

    @pl.when(side == 0)
    def _():
        for layer in range(layers):
            tile_copy(layer).start()

    for layer in range(layers):
        cut(own_cols, layer, cut_own)
    phase_turned = phase[...].T
    work[count] = jnp.concatenate([jnp.cos(phase_turned), jnp.sin(phase_turned)], axis=1)
    for p in range(count):
        turned[p] = measured[p].T

    @pl.when(side == 0)
    def _():
        for layer in range(layers):
            tile_copy(layer).wait_send()
        pl.semaphore_signal(go, inc=1, device_id={"slab": partner}, device_id_type=MESH)

    @pl.when(side == 1)
    def _():
        pl.semaphore_wait(go, 1)
        for layer in range(layers):
            tile_copy(layer).start()

    def cross_copy(step, layer):
        block = patches.at[first_own + layer]
        return remote(
            block, block, cross_send.at[step - 1, layer], cross_recv.at[step - 1, layer],
            slab=lax.rem(group + step, groups) * 2 + side,
        )

    def origin(step, of_side):
        return (lax.rem(group + groups - step, groups) * 2 + of_side) * layers

    def cross_arrival(step, layer):
        block = patches.at[origin(step, side) + layer]
        return remote(
            block, block, cross_send.at[step - 1, layer], cross_recv.at[step - 1, layer],
            slab=lax.rem(group + step, groups) * 2 + side,
        )

    def pair_copy(step, layer):
        block = patches.at[origin(step, side) + layer]
        return remote(
            block, block, pair_send.at[step, layer], pair_recv.at[step, layer], slab=partner
        )

    def pair_arrival(step, layer):
        block = patches.at[origin(step, 1 - side) + layer]
        return remote(
            block, block, pair_send.at[step, layer], pair_recv.at[step, layer], slab=partner
        )

    def take_rows(layer):
        tile_copy(layer).wait_recv()
        for p in range(count):
            both = jnp.concatenate([cut_own[layer, p], low[layer, p]], axis=0)
            pick = one_hot((window, 2 * window), 1, own_rows[p])
            patches[first_own + layer, p] = jnp.dot(
                pick, both, preferred_element_type=F32
            ).astype(BF16)
        pair_copy(0, layer).start()
        for step in range(1, groups):
            cross_copy(step, layer).start()

    take_rows(0)

    @pl.when(group > 0)
    def _():
        for layer in range(1, layers):
            take_rows(layer)

    def arrive(j):
        owner, layer = j // layers, lax.rem(j, layers)
        of_group, of_side = owner // 2, lax.rem(owner, 2)
        step = lax.rem(group - of_group + groups, groups)

        @pl.when((of_side == side) & (of_group != group))
        def _():
            cross_arrival(step, layer).wait_recv()
            pair_copy(step, layer).start()

        @pl.when(of_side != side)
        def _():
            pair_arrival(step, layer).wait_recv()

    table.wait()
    run = functools.partial(transform, right=right, window=window)
    start = (probe[0].astype(F32), probe[1].astype(F32))
    store(psi, 0, [start] * count)

    def propagator():
        return halves(work[count], window)

    def forward(j, carried):
        @pl.when((group == 0) & (j >= 1) & (j < layers))
        def _():
            take_rows(j)

        arrive(j)
        chi = [
            times(a, b)
            for a, b in zip(load(psi, j, count, window), load(patches, j, count, window))
        ]
        moved = run(chi)
        prop = propagator()
        back = run([conj(times(prop, f)) for f in moved])
        store(psi, j + 1, [conj(f) for f in back])
        return carried

    lax.fori_loop(0, last, forward, 0)
    arrive(last)
    chi = [
        times(a, b)
        for a, b in zip(load(psi, last, count, window), load(patches, last, count, window))
    ]
    far = run(chi)
    shaped = []
    for p, (re, im) in enumerate(far):
        misfit = re * re + im * im - turned[p]
        shaped.append((misfit * re, -(misfit * im)))
    grad = [conj(f) for f in run(shaped)]
    for p in range(count):
        work[p] = jnp.concatenate(grad[p], axis=1)

    def spill_copy(layer, p):
        return remote(
            spill.at[layer, p], spilled.at[layer, p],
            back_send.at[layer, p], back_recv.at[layer, p], tile=after,
        )

    def own_term(j):
        @pl.when((j >= first_own) & (j < first_own + layers))
        def _():
            layer = j - first_own
            for p in range(count):
                term = jnp.concatenate(
                    conj_times(halves(psi[j, p], window), halves(work[p], window)), axis=1
                )
                parts = jnp.concatenate(split(term), axis=0)
                pick = one_hot((window, window), 0, own_rows[p] - window)
                spill[layer, p] = jnp.dot(
                    jnp.concatenate([pick, pick], axis=1), parts, preferred_element_type=F32
                ).astype(BF16)
                spill_copy(layer, p).start()
                pick = one_hot((window, window), 0, own_rows[p])
                terms[layer, p] = jnp.dot(
                    jnp.concatenate([pick, pick], axis=1), parts, preferred_element_type=F32
                )

    def backward(i, carried):
        j = last - i
        own_term(j)
        grads = [halves(work[p], window) for p in range(count)]
        inner = [conj_times(a, b) for a, b in zip(load(patches, j, count, window), grads)]
        moved = run(inner)
        prop = propagator()
        back = run([conj(conj_times(prop, f)) for f in moved])
        for p in range(count):
            work[p] = jnp.concatenate(conj(back[p]), axis=1)
        return carried

    lax.fori_loop(0, last - first_own, backward, 0)
    own_term(first_own)

    own_place = jnp.concatenate([one_hot((window, columns), 1, c) for c in own_cols], axis=0)
    prior_place = jnp.concatenate([one_hot((window, columns), 1, c) for c in prior_cols], axis=0)

    def by_part(ref, layer):
        wide = [halves(ref[layer, p], window) for p in range(count)]
        return jnp.concatenate(
            [jnp.concatenate([w[part] for w in wide], axis=1) for part in range(2)], axis=0
        )

    for layer in reversed(range(layers)):
        high, low_part = split(by_part(terms, layer))
        total = jnp.dot(high, own_place, preferred_element_type=F32)
        total += jnp.dot(low_part, own_place, preferred_element_type=F32)
        for p in range(count):
            spill_copy(layer, p).wait_recv()
        total += jnp.dot(by_part(spilled, layer), prior_place, preferred_element_type=F32)
        out[0, layer] = total[:window].astype(out.dtype)
        out[1, layer] = total[window:].astype(out.dtype)

    @pl.when(side == 1)
    def _():
        for layer in range(layers):
            tile_copy(layer).wait_send()

    for layer in range(layers):
        for p in range(count):
            spill_copy(layer, p).wait_send()
        for step in range(1, groups):
            cross_copy(step, layer).wait_send()
        for step in range(groups):
            pair_copy(step, layer).wait_send()


def body(object_field, probe_wave, prop_phase, intensity, patch_rows, patch_cols):
    window = probe_wave.shape[1]
    layers = object_field.shape[1]
    count = intensity.shape[0]
    tiles, sections = lax.axis_size("tile"), lax.axis_size("slab")
    slices = sections * layers
    groups = sections // 2
    right = fourier_parts(window)
    wide = (layers, count, window, 2 * window)
    dma = pltpu.SemaphoreType.DMA
    return pl.pallas_call(
        functools.partial(kernel, tiles, sections),
        out_shape=jax.ShapeDtypeStruct(object_field.shape, BF16),
        in_specs=[pl.BlockSpec(memory_space=pltpu.SMEM)] * 2
        + [pl.BlockSpec(memory_space=pltpu.VMEM)] * 4
        + [pl.BlockSpec(memory_space=pl.ANY)],
        out_specs=pl.BlockSpec(memory_space=pltpu.VMEM),
        scratch_shapes=[
            pltpu.VMEM(wide, BF16),
            pltpu.VMEM(wide, BF16),
            pltpu.VMEM(wide, BF16),
            pltpu.VMEM((slices,) + wide[1:], BF16),
            pltpu.VMEM((slices,) + wide[1:], F32),
            pltpu.VMEM((count + 1, window, 2 * window), F32),
            pltpu.VMEM(wide, F32),
            pltpu.VMEM(wide, BF16),
            pltpu.VMEM(wide, BF16),
            pltpu.VMEM(right.shape, BF16),
            pltpu.VMEM(intensity.shape, F32),
            dma((layers,)),
            dma((layers,)),
            dma((groups - 1, layers)),
            dma((groups - 1, layers)),
            dma((groups, layers)),
            dma((groups, layers)),
            dma((layers, count)),
            dma((layers, count)),
            dma(()),
            pltpu.SemaphoreType.REGULAR,
        ],
        compiler_params=pltpu.CompilerParams(
            collective_id=0, has_side_effects=True, vmem_limit_bytes=60 * 1024 * 1024
        ),
    )(
        patch_rows, patch_cols, object_field, probe_wave, prop_phase, intensity,
        jnp.asarray(right),
    )


def solution(mesh):
    return jax.shard_map(
        body,
        mesh=mesh,
        in_specs=(P(None, "slab", "tile", None), P(), P(), P("tile", None, None), P(), P()),
        out_specs=P(None, "slab", "tile", None),
        check_vma=False,
    )
```

profile of v0, /device:TPU:0, one launch (start us, length us, event | category | flops | bytes accessed | tf_op | source)
XLA Modules:
  0.0 43.4 jit_solution(2649557367799685235)
XLA Ops:
  0.0 41.5 %shard_map.73 = bf16[2,2,128,512]{3,2,1,0:T(8,128)(2,1)} custom-call(s32[16]{0:T(128)} %row_ref.1, s32[16]{0:T(128)} %col_ref.1, bf16[2,2,128,512]{3,2,1,0:T(8,128)(2,1)} %obj.1, bf16[2,128,128]{2,1,0:T(8,128)(2,1)} %probe.1, f32[128,128]{1,0:T(8,128)} %phase.1, f32[2,128,128]{2,1,0:T(8,128)} %measured.1, bf16[768,256]{1,0:T(8,128)(2,1)} %constant.2.clone.right_in), custom_call_target="tpu_custom_call" | custom-call | tf_op jit(solution)/shard_map/pallas_call | solution.py:345
  41.5 1.9 %copy.9 = bf16[2,2,128,512]{3,2,1,0:T(8,128)(2,1)} copy(bf16[2,2,128,512]{3,2,1,0:T(8,128)(2,1)} %shard_map.73) | data formatting | bytes 1048576
where the time goes:
time: 43.6 us; the launch traced here: 43.4 us
  Pallas kernels  41.5 us (95%)
  local copies, waits for them, and re-layouts  1.87 us (4%)
    pallas_call x1, Pallas kernels, body(): pl.pallas_call(functools.partial(kernel, tiles, sections), out_shape=jax....  41.5 us
    unnamed x1, local copies, waits for them, and re-layouts  1.87 us

commit v1 on v0

v1 whole, which is shorter than its diff:
```python
import functools
import math

import jax
import jax.numpy as jnp
import numpy as np
from jax import lax
from jax.experimental import pallas as pl
from jax.experimental.pallas import tpu as pltpu
from jax.sharding import PartitionSpec as P

F32 = jnp.float32
BF16 = jnp.bfloat16


def fourier_parts(window):
    index = np.arange(window)
    angle = (index[:, None] * index[None, :] % window) * (-2.0 * math.pi / window)
    real = np.cos(angle) / math.sqrt(window)
    imag = np.sin(angle) / math.sqrt(window)
    big = np.block([[real, imag], [-imag, real]]).astype(np.float32)
    high = big.astype(BF16)
    low = (big - high.astype(np.float32)).astype(BF16)
    return np.concatenate([high, high, low], axis=0)


def split(value):
    high = value.astype(BF16)
    return high, (value - high.astype(F32)).astype(BF16)


def from_right(field, right, window):
    high, low = split(jnp.concatenate(field, axis=1))
    lhs = jnp.concatenate([high, low, high], axis=1)
    rows = lhs.shape[0] // 2
    table = right[...]
    product = jnp.concatenate(
        [
            jnp.dot(lhs[:rows], table, preferred_element_type=F32),
            jnp.dot(lhs[rows:], table, preferred_element_type=F32),
        ],
        axis=0,
    )
    return product[:, :window], product[:, window:]


def transform(field, right, window):
    first = [from_right(f, right, window) for f in field]
    return [from_right((re.T, im.T), right, window) for re, im in first]


def times(a, b):
    return a[0] * b[0] - a[1] * b[1], a[0] * b[1] + a[1] * b[0]


def conj_times(a, b):
    return a[0] * b[0] + a[1] * b[1], a[0] * b[1] - a[1] * b[0]


def conj(a):
    return a[0], -a[1]


MESH = pl.DeviceIdType.MESH


def one_hot(shape, along, offset):
    here = lax.broadcasted_iota(jnp.int32, shape, along)
    there = lax.broadcasted_iota(jnp.int32, shape, 1 - along)
    return jnp.where(here == there + offset, 1.0, 0.0).astype(BF16)


def halves(block, window):
    return block[:, :window], block[:, window:]


def wide(field):
    return jnp.concatenate(field, axis=1)


def kernel(
    tiles, sections, row_ref, col_ref, obj, probe, phase, measured, right_in, out,
    place, cut_low, cut_high, cut_give, both, patches, psi, work, prop, seen, turned, stage, landed, right,
    low_send, high_send, give_send, part_recv, give_recv, cross_send, cross_recv,
    seen_send, seen_recv, near_send, near_recv, far_send, far_recv, table_sem,
):
    layers, window, columns = obj.shape[1], obj.shape[2], obj.shape[3]
    count, slices = measured.shape[0], patches.shape[0]
    half = count // 2
    groups = sections // 2
    owned = 2 * layers
    last = slices - 1
    tile = lax.axis_index("tile")
    slab = lax.axis_index("slab")
    after, prior = lax.rem(tile + 1, tiles), lax.rem(tile + tiles - 1, tiles)
    group, side = slab // 2, lax.rem(slab, 2)
    partner = slab + 1 - 2 * side
    first_own = group * owned
    base = jnp.where(side == 0, tile, prior)
    beyond = jnp.where(side == 0, after, prior)

    def remote(src, dst, send, recv, **device):
        return pltpu.make_async_remote_copy(
            src_ref=src, dst_ref=dst, send_sem=send, recv_sem=recv,
            device_id=device, device_id_type=MESH,
        )

    barrier = pltpu.get_barrier_semaphore()
    greeted = [{"tile": to, "slab": 2 * group + s} for to in (after, prior) for s in range(2)]
    greeted.append({"slab": partner})
    for step in range(1, groups):
        greeted.append({"slab": lax.rem(group + step, groups) * 2 + side})
    for device in greeted:
        pl.semaphore_signal(barrier, inc=1, device_id=device, device_id_type=MESH)
    table = pltpu.make_async_copy(right_in, right, table_sem)
    table.start()

    starts = [prior * count, tile * count + half, tile * count, prior * count + half]
    for slot, start in enumerate(starts):
        for q in range(half):
            place[slot, q] = one_hot((window, columns), 1, col_ref[start + q])

    def cut(layer, pick):
        rows = jnp.concatenate([obj[0, layer], obj[1, layer]], axis=0)
        got = lax.dot_general(
            rows, pick, (((1,), (1,)), ((), ())), preferred_element_type=F32
        ).astype(BF16)
        return wide((got[:window], got[window:]))

    def low_copy(layer, q):
        return remote(
            cut_low.at[layer, q], both.at[side * layers + layer, q, 1],
            low_send.at[layer, q], part_recv.at[side * layers + layer, q],
            tile=prior, slab=2 * group,
        )

    def high_copy(layer, q):
        return remote(
            cut_high.at[layer, q], both.at[side * layers + layer, q, 0],
            high_send.at[layer, q], part_recv.at[side * layers + layer, q],
            tile=after, slab=2 * group + 1,
        )

    def give_copy(layer, q):
        return remote(
            cut_give.at[layer, q], both.at[side * layers + layer, q, 1 - side],
            give_send.at[layer, q], give_recv.at[layer, q], slab=partner,
        )

    def seen_copy(q):
        return remote(
            measured.at[half + q], seen.at[q], seen_send.at[q], seen_recv.at[q], tile=after
        )

    for layer in range(layers):
        for q in range(half):
            cut_low[layer, q] = cut(layer, place[0, q])
            cut_high[layer, q] = cut(layer, place[1, q])
        if layer == 0:
            pl.semaphore_wait(barrier, len(greeted))
        for q in range(half):
            low_copy(layer, q).start()
            high_copy(layer, q).start()
    for layer in range(layers):
        for q in range(half):
            cut_give[layer, q] = cut(layer, place[3 - side, q])
            give_copy(layer, q).start()
    for layer in range(layers):
        for q in range(half):
            both[side * layers + layer, q, side] = cut(layer, place[2 + side, q])

    @pl.when(side == 1)
    def _():
        for q in range(half):
            seen_copy(q).start()

    my_rows = [row_ref[base * count + side * half + q] for q in range(half)]
    phase_turned = phase[...].T
    prop[...] = wide((jnp.cos(phase_turned), jnp.sin(phase_turned)))

    def cross_copy(step, at):
        block = patches.at[first_own + at]
        return remote(
            block, block, cross_send.at[step - 1, at], cross_recv.at[step - 1, at],
            slab=lax.rem(group + step, groups) * 2 + side,
        )

    def cross_arrival(step, j, at):
        block = patches.at[j]
        return remote(
            block, block, cross_send.at[step - 1, at], cross_recv.at[step - 1, at],
            slab=lax.rem(group + step, groups) * 2 + side,
        )

    def take_rows(at):
        owner = at // layers
        for q in range(half):
            remote(
                cut_low.at[0, q], both.at[at, q, 1 - side],
                low_send.at[0, q], part_recv.at[at, q], slab=partner,
            ).wait_recv()

        @pl.when(owner != side)
        def _():
            for q in range(half):
                layer = lax.rem(at, layers)
                remote(
                    cut_give.at[0, q], both.at[at, q, side],
                    give_send.at[0, q], give_recv.at[layer, q], slab=partner,
                ).wait_recv()

        for q in range(half):
            pick = one_hot((window, 2 * window), 1, my_rows[q])
            rows = both[at, q].reshape(2 * window, 2 * window)
            patches[first_own + at, q] = jnp.dot(
                pick, rows, preferred_element_type=F32
            ).astype(BF16)
        for step in range(1, groups):
            cross_copy(step, at).start()

    @pl.when(group > 0)
    def _():
        for at in range(owned):
            take_rows(at)

    def arrive(j):
        of_group, at = j // owned, lax.rem(j, owned)
        step = lax.rem(group - of_group + groups, groups)

        @pl.when(of_group != group)
        def _():
            cross_arrival(step, j, at).wait_recv()

    table.wait()
    run = functools.partial(transform, right=right, window=window)
    start = (probe[0].astype(F32), probe[1].astype(F32))
    for q in range(half):
        psi[0, q] = wide(start)

    def patch(j):
        return [halves(patches[j, q].astype(F32), window) for q in range(half)]

    def waves(ref, j):
        return [halves(ref[j, q], window) for q in range(half)]

    def forward(j, carried):
        @pl.when((group == 0) & (j < owned))
        def _():
            take_rows(j)

        arrive(j)
        chi = [times(a, b) for a, b in zip(waves(psi, j), patch(j))]
        moved = run(chi)
        pace = halves(prop[...], window)
        back = run([conj(times(pace, f)) for f in moved])
        for q in range(half):
            psi[j + 1, q] = wide(conj(back[q]))
        return carried

    lax.fori_loop(0, last, forward, 0)

    @pl.when(side == 0)
    def _():
        for q in range(half):
            turned[q] = measured[q].T

    @pl.when(side == 1)
    def _():
        for q in range(half):
            seen_copy(q).wait_recv()
            turned[q] = seen[q].T

    @pl.when((group == 0) & (last < owned))
    def _():
        take_rows(last)

    arrive(last)
    chi = [times(a, b) for a, b in zip(waves(psi, last), patch(last))]
    far = run(chi)
    shaped = []
    for q, (re, im) in enumerate(far):
        misfit = re * re + im * im - turned[q]
        shaped.append((misfit * re, -(misfit * im)))
    grad = [conj(f) for f in run(shaped)]
    for q in range(half):
        work[q] = wide(grad[q])

    def near_copy(at, q):
        return remote(
            stage.at[at, q, side], landed.at[lax.rem(at, layers), 2 + side, q],
            near_send.at[lax.rem(at, layers), q], near_recv.at[lax.rem(at, layers), q], slab=partner,
        )

    def far_copy(at, q):
        return remote(
            stage.at[at, q, 1 - side], landed.at[lax.rem(at, layers), side, q],
            far_send.at[at, q], far_recv.at[side, lax.rem(at, layers), q],
            tile=beyond, slab=2 * group + at // layers,
        )

    def own_term(j):
        @pl.when(j < first_own + owned)
        def _():
            at = j - first_own
            for q in range(half):
                term = wide(conj_times(halves(psi[j, q], window), halves(work[q], window)))
                pick = one_hot((2 * window, window), 0, my_rows[q])
                placed = jnp.dot(
                    pick, term.astype(BF16), preferred_element_type=F32
                ).astype(BF16)
                stage[at, q] = placed.reshape(2, window, 2 * window)
                far_copy(at, q).start()

            @pl.when(at // layers != side)
            def _():
                for q in range(half):
                    near_copy(at, q).start()

    def backward(i, carried):
        j = last - i
        own_term(j)
        grads = [halves(work[q], window) for q in range(half)]
        inner = [conj_times(a, b) for a, b in zip(patch(j), grads)]
        moved = run(inner)
        pace = halves(prop[...], window)
        back = run([conj(conj_times(pace, f)) for f in moved])
        for q in range(half):
            work[q] = wide(conj(back[q]))
        return carried

    lax.fori_loop(0, last - first_own, backward, 0)
    own_term(first_own)

    def far_arrival(layer, of_side, q):
        return remote(
            stage.at[0, q, 0], landed.at[layer, of_side, q],
            far_send.at[0, q], far_recv.at[of_side, layer, q], slab=partner,
        )

    def near_arrival(layer, q):
        return remote(
            stage.at[0, q, 0], landed.at[layer, 3 - side, q],
            near_send.at[layer, q], near_recv.at[layer, q], slab=partner,
        )

    all_place = place[...].reshape(4 * half * window, columns)
    for layer in reversed(range(layers)):
        for q in range(half):
            landed[layer, 2 + side, q] = stage[side * layers + layer, q, side]
            near_arrival(layer, q).wait_recv()
            for of_side in range(2):
                far_arrival(layer, of_side, q).wait_recv()
        blocks = [halves(landed[layer, slot, q], window) for slot in range(4) for q in range(half)]
        both_parts = jnp.concatenate(
            [jnp.concatenate([b[part] for b in blocks], axis=1) for part in range(2)], axis=0
        )
        total = jnp.dot(both_parts, all_place, preferred_element_type=F32).astype(out.dtype)
        out[0, layer] = total[:window]
        out[1, layer] = total[window:]

    @pl.when(side == 1)
    def _():
        for q in range(half):
            seen_copy(q).wait_send()

    for q in range(half):
        for layer in range(layers):
            low_copy(layer, q).wait_send()
            high_copy(layer, q).wait_send()
            give_copy(layer, q).wait_send()
            near_copy((1 - side) * layers + layer, q).wait_send()
        for at in range(owned):
            far_copy(at, q).wait_send()
    for at in range(owned):
        for step in range(1, groups):
            cross_copy(step, at).wait_send()


def body(object_field, probe_wave, prop_phase, intensity, patch_rows, patch_cols):
    window = probe_wave.shape[1]
    layers, columns = object_field.shape[1], object_field.shape[3]
    half = intensity.shape[0] // 2
    tiles, sections = lax.axis_size("tile"), lax.axis_size("slab")
    slices = sections * layers
    groups = sections // 2
    owned = 2 * layers
    right = fourier_parts(window)
    block = (window, 2 * window)
    dma = pltpu.SemaphoreType.DMA
    return pl.pallas_call(
        functools.partial(kernel, tiles, sections),
        out_shape=jax.ShapeDtypeStruct(object_field.shape, BF16),
        in_specs=[pl.BlockSpec(memory_space=pltpu.SMEM)] * 2
        + [pl.BlockSpec(memory_space=pltpu.VMEM)] * 4
        + [pl.BlockSpec(memory_space=pl.ANY)],
        out_specs=pl.BlockSpec(memory_space=pltpu.VMEM),
        scratch_shapes=[
            pltpu.VMEM((4, half, window, columns), BF16),
            pltpu.VMEM((layers, half) + block, BF16),
            pltpu.VMEM((layers, half) + block, BF16),
            pltpu.VMEM((layers, half) + block, BF16),
            pltpu.VMEM((owned, half, 2) + block, BF16),
            pltpu.VMEM((slices, half) + block, BF16),
            pltpu.VMEM((slices, half) + block, F32),
            pltpu.VMEM((half,) + block, F32),
            pltpu.VMEM(block, F32),
            pltpu.VMEM((half, window, window), F32),
            pltpu.VMEM((half, window, window), F32),
            pltpu.VMEM((owned, half, 2) + block, BF16),
            pltpu.VMEM((layers, 4, half) + block, BF16),
            pltpu.VMEM(right.shape, BF16),
            dma((layers, half)),
            dma((layers, half)),
            dma((layers, half)),
            dma((owned, half)),
            dma((layers, half)),
            dma((groups - 1, owned)),
            dma((groups - 1, owned)),
            dma((half,)),
            dma((half,)),
            dma((layers, half)),
            dma((layers, half)),
            dma((owned, half)),
            dma((2, layers, half)),
            dma(()),
        ],
        compiler_params=pltpu.CompilerParams(
            collective_id=0, has_side_effects=True, vmem_limit_bytes=60 * 1024 * 1024
        ),
    )(
        patch_rows, patch_cols, object_field, probe_wave, prop_phase, intensity,
        jnp.asarray(right),
    )


def solution(mesh):
    return jax.shard_map(
        body,
        mesh=mesh,
        in_specs=(P(None, "slab", "tile", None), P(), P(), P("tile", None, None), P(), P()),
        out_specs=P(None, "slab", "tile", None),
        check_vma=False,
    )
```

time: 43.6 us -> 37.4 us (0.86)
  Pallas kernels: 41.5 us -> 35.3 us
    pallas_call x1, Pallas kernels: 41.5 us -> 35.3 us  [body(): pl.pallas_call(functools.partial(kernel, tiles, sections), out_shape=jax....]
where the time goes in v1:
time: 37.4 us; the launch traced here: 37.2 us
  Pallas kernels  35.3 us (94%)
  local copies, waits for them, and re-layouts  1.87 us (5%)
    pallas_call x1, Pallas kernels, body(): pl.pallas_call(functools.partial(kernel, tiles, sections), out_shape=jax....  35.3 us
    unnamed x1, local copies, waits for them, and re-layouts  1.87 us

profile of v1, /device:TPU:0, one launch (start us, length us, event | category | flops | bytes accessed | tf_op | source)
XLA Modules:
  0.0 37.2 jit_solution(518175927687010244)
XLA Ops:
  0.0 35.3 %shard_map.73 = bf16[2,2,128,512]{3,2,1,0:T(8,128)(2,1)} custom-call(s32[16]{0:T(128)} %row_ref.1, s32[16]{0:T(128)} %col_ref.1, bf16[2,2,128,512]{3,2,1,0:T(8,128)(2,1)} %obj.1, bf16[2,128,128]{2,1,0:T(8,128)(2,1)} %probe.1, f32[128,128]{1,0:T(8,128)} %phase.1, f32[2,128,128]{2,1,0:T(8,128)} %measured.1, bf16[768,256]{1,0:T(8,128)(2,1)} %constant.2.clone.right_in), custom_call_target="tpu_custom_call" | custom-call | tf_op jit(solution)/shard_map/pallas_call | solution.py:390
  35.3 1.9 %copy.9 = bf16[2,2,128,512]{3,2,1,0:T(8,128)(2,1)} copy(bf16[2,2,128,512]{3,2,1,0:T(8,128)(2,1)} %shard_map.73) | data formatting | bytes 1048576

commit v2 on v1

v2 whole, which is shorter than its diff:
```python
import functools
import math

import jax
import jax.numpy as jnp
import numpy as np
from jax import lax
from jax.experimental import pallas as pl
from jax.experimental.pallas import tpu as pltpu
from jax.sharding import PartitionSpec as P

F32 = jnp.float32
BF16 = jnp.bfloat16


def fourier_parts(window):
    index = np.arange(window)
    angle = (index[:, None] * index[None, :] % window) * (-2.0 * math.pi / window)
    real = np.cos(angle) / math.sqrt(window)
    imag = np.sin(angle) / math.sqrt(window)
    big = np.block([[real, imag], [-imag, real]]).astype(np.float32)
    high = big.astype(BF16)
    low = (big - high.astype(np.float32)).astype(BF16)
    left = np.block([[real, -imag], [imag, real]]).astype(np.float32)
    left_high = left.astype(BF16)
    left_low = (left - left_high.astype(np.float32)).astype(BF16)
    w = window
    return np.concatenate(
        [high, high, low, left_high[:w], left_low[:w], left_high[w:], left_low[w:]], axis=0
    )


def split(value):
    high = value.astype(BF16)
    return high, (value - high.astype(F32)).astype(BF16)


def from_right(field, right, window):
    high, low = split(jnp.concatenate(field, axis=1))
    wide_rows, table_rows = high.shape[0] // 2, 2 * window
    parts = []
    for at in (0, wide_rows):
        upper, lower = high[at : at + wide_rows], low[at : at + wide_rows]
        main = jnp.dot(
            jnp.concatenate([upper, lower], axis=0), right[:table_rows], preferred_element_type=F32
        )
        rest = jnp.dot(upper, right[2 * table_rows : 3 * table_rows], preferred_element_type=F32)
        parts.append(main[:wide_rows] + main[wide_rows:] + rest)
    product = jnp.concatenate(parts, axis=0)
    return product[:, :window], product[:, window:]


def from_left(field, right, window):
    high, low = split(jnp.concatenate(field, axis=0))
    data = jnp.concatenate([high, low], axis=1)
    table_rows = 2 * window
    out = []
    for part in range(2):
        rows = right[pl.ds(3 * table_rows + part * table_rows, table_rows)]
        got = jnp.dot(rows, data, preferred_element_type=F32)
        out.append(got[:window, :window] + got[:window, window:] + got[window:, :window])
    return out[0], out[1]


def transform(field, right, window):
    first = [from_right(f, right, window) for f in field]
    return [from_left(f, right, window) for f in first]


def times(a, b):
    return a[0] * b[0] - a[1] * b[1], a[0] * b[1] + a[1] * b[0]


def conj_times(a, b):
    return a[0] * b[0] + a[1] * b[1], a[0] * b[1] - a[1] * b[0]


def conj(a):
    return a[0], -a[1]


MESH = pl.DeviceIdType.MESH


def one_hot(shape, along, offset):
    here = lax.broadcasted_iota(jnp.int32, shape, along)
    there = lax.broadcasted_iota(jnp.int32, shape, 1 - along)
    return jnp.where(here == there + offset, 1.0, 0.0).astype(BF16)


def halves(block, window):
    return block[:, :window], block[:, window:]


def kernel(
    tiles, sections, row_in, col_in, obj_in, probe_in, phase_in, measured_in, right_in, out,
    row_ref, col_ref, obj, probe, phase, measured,
    place, cut_low, cut_high, cut_give, both, patches, psi, work, prop, seen, stage, landed, right,
    load_sem, obj_sem,
    low_send, high_send, give_send, part_recv, give_recv, cross_send, cross_recv,
    seen_send, seen_recv, near_send, near_recv, far_send, far_recv,
):
    layers, window, columns = obj.shape[1], obj.shape[2], obj.shape[3]
    count, slices = measured.shape[0], patches.shape[0]
    half = count // 2
    groups = sections // 2
    owned = 2 * layers
    last = slices - 1
    tile = lax.axis_index("tile")
    slab = lax.axis_index("slab")
    after, prior = lax.rem(tile + 1, tiles), lax.rem(tile + tiles - 1, tiles)
    group, side = slab // 2, lax.rem(slab, 2)
    partner = slab + 1 - 2 * side
    first_own = group * owned
    base = jnp.where(side == 0, tile, prior)
    beyond = jnp.where(side == 0, after, prior)
    pieces = [(q, c) for q in range(half) for c in range(2)]

    def remote(src, dst, send, recv, **device):
        return pltpu.make_async_remote_copy(
            src_ref=src, dst_ref=dst, send_sem=send, recv_sem=recv,
            device_id=device, device_id_type=MESH,
        )

    barrier = pltpu.get_barrier_semaphore()
    greeted = [{"tile": to, "slab": 2 * group + s} for to in (after, prior) for s in range(2)]
    greeted.append({"slab": partner})
    for step in range(1, groups):
        greeted.append({"slab": lax.rem(group + step, groups) * 2 + side})
    for device in greeted:
        pl.semaphore_signal(barrier, inc=1, device_id=device, device_id_type=MESH)

    loads = [
        pltpu.make_async_copy(src, dst, load_sem.at[k])
        for k, (src, dst) in enumerate(
            [(col_in, col_ref), (row_in, row_ref), (phase_in, phase), (probe_in, probe),
             (right_in, right), (measured_in, measured)]
        )
    ]
    obj_loads = [
        pltpu.make_async_copy(obj_in.at[:, layer], obj.at[:, layer], obj_sem.at[layer])
        for layer in range(layers)
    ]
    loads[0].start()
    for copy in obj_loads + loads[1:]:
        copy.start()

    loads[0].wait()
    starts = [prior * count, tile * count + half, tile * count, prior * count + half]
    for slot, start in enumerate(starts):
        for q in range(half):
            place[slot, q] = one_hot((window, columns), 1, col_ref[start + q])

    def cut(layer, pick, target):
        for c in range(2):
            target[c] = lax.dot_general(
                obj[c, layer], pick, (((1,), (1,)), ((), ())), preferred_element_type=F32
            ).astype(BF16)

    def low_copy(layer, q, c):
        return remote(
            cut_low.at[layer, q, c], both.at[side * layers + layer, q, c, 1],
            low_send.at[layer, q, c], part_recv.at[side * layers + layer, q, c],
            tile=prior, slab=2 * group,
        )

    def high_copy(layer, q, c):
        return remote(
            cut_high.at[layer, q, c], both.at[side * layers + layer, q, c, 0],
            high_send.at[layer, q, c], part_recv.at[side * layers + layer, q, c],
            tile=after, slab=2 * group + 1,
        )

    def give_copy(layer, q, c):
        return remote(
            cut_give.at[layer, q, c], both.at[side * layers + layer, q, c, 1 - side],
            give_send.at[layer, q, c], give_recv.at[layer, q, c], slab=partner,
        )

    def seen_copy(q):
        return remote(
            measured.at[half + q], seen.at[q], seen_send.at[q], seen_recv.at[q], tile=after
        )

    for layer in range(layers):
        obj_loads[layer].wait()
        for q in range(half):
            cut(layer, place[0, q], cut_low.at[layer, q])
            cut(layer, place[1, q], cut_high.at[layer, q])
    pl.semaphore_wait(barrier, len(greeted))
    for layer in range(layers):
        for q, c in pieces:
            low_copy(layer, q, c).start()
            high_copy(layer, q, c).start()
    for layer in range(layers):
        for q in range(half):
            cut(layer, place[3 - side, q], cut_give.at[layer, q])
        for q, c in pieces:
            give_copy(layer, q, c).start()
    for layer in range(layers):
        for q, c in pieces:
            both[side * layers + layer, q, c, side] = lax.dot_general(
                obj[c, layer], place[2 + side, q], (((1,), (1,)), ((), ())),
                preferred_element_type=F32,
            ).astype(BF16)

    for copy in loads[1:]:
        copy.wait()
    my_rows = [row_ref[base * count + side * half + q] for q in range(half)]
    prop[0] = jnp.cos(phase[...])
    prop[1] = jnp.sin(phase[...])

    def cross_copy(step, at, c):
        block = patches.at[first_own + at, c]
        return remote(
            block, block, cross_send.at[step - 1, at, c], cross_recv.at[step - 1, at, c],
            slab=lax.rem(group + step, groups) * 2 + side,
        )

    def cross_arrival(step, j, at, c):
        block = patches.at[j, c]
        return remote(
            block, block, cross_send.at[step - 1, at, c], cross_recv.at[step - 1, at, c],
            slab=lax.rem(group + step, groups) * 2 + side,
        )

    def take_rows(at, c):
        owner, layer = at // layers, lax.rem(at, layers)
        for q in range(half):
            remote(
                cut_low.at[0, q, c], both.at[at, q, c, 1 - side],
                low_send.at[0, q, c], part_recv.at[at, q, c], slab=partner,
            ).wait_recv()

        @pl.when(owner != side)
        def _():
            for q in range(half):
                remote(
                    cut_give.at[0, q, c], both.at[at, q, c, side],
                    give_send.at[0, q, c], give_recv.at[layer, q, c], slab=partner,
                ).wait_recv()

        for q in range(half):
            pick = one_hot((window, 2 * window), 1, my_rows[q])
            rows = both[at, q, c].reshape(2 * window, window)
            patches[first_own + at, c, q] = jnp.dot(
                pick, rows, preferred_element_type=F32
            ).astype(BF16)
        for step in range(1, groups):
            cross_copy(step, at, c).start()

    @pl.when(group > 0)
    def _():
        for layer in range(layers):
            for c in range(2):
                for owner in range(2):
                    take_rows(owner * layers + layer, c)

    def arrive(j):
        of_group, at = j // owned, lax.rem(j, owned)
        step = lax.rem(group - of_group + groups, groups)

        @pl.when(of_group != group)
        def _():
            for c in range(2):
                cross_arrival(step, j, at, c).wait_recv()

    run = functools.partial(transform, right=right, window=window)
    for q in range(half):
        for c in range(2):
            psi[0, q, c] = probe[c].astype(F32)

    def patch(j):
        return [(patches[j, 0, q].astype(F32), patches[j, 1, q].astype(F32)) for q in range(half)]

    def pair(ref, q):
        return ref[q, 0], ref[q, 1]

    def waves(j):
        return [(psi[j, q, 0], psi[j, q, 1]) for q in range(half)]

    def forward(j, carried):
        @pl.when((group == 0) & (j < layers))
        def _():
            for c in range(2):
                take_rows(j, c)
                take_rows(j + layers, c)

        @pl.when((side == 1) & (j == layers))
        def _():
            for q in range(half):
                seen_copy(q).start()

        arrive(j)
        chi = [times(a, b) for a, b in zip(waves(j), patch(j))]
        moved = run(chi)
        pace = (prop[0], prop[1])
        back = run([conj(times(pace, f)) for f in moved])
        for q in range(half):
            psi[j + 1, q, 0] = back[q][0]
            psi[j + 1, q, 1] = -back[q][1]
        return carried

    lax.fori_loop(0, last, forward, 0)

    @pl.when(side == 0)
    def _():
        for q in range(half):
            seen[q] = measured[q]

    @pl.when(side == 1)
    def _():
        for q in range(half):
            seen_copy(q).wait_recv()

    arrive(last)
    chi = [times(a, b) for a, b in zip(waves(last), patch(last))]
    far = run(chi)
    shaped = []
    for q, (re, im) in enumerate(far):
        misfit = re * re + im * im - seen[q]
        shaped.append((misfit * re, -(misfit * im)))
    grad = [conj(f) for f in run(shaped)]
    for q in range(half):
        work[q, 0], work[q, 1] = grad[q]

    def near_copy(at, q):
        return remote(
            stage.at[at, q, side], landed.at[lax.rem(at, layers), 2 + side, q],
            near_send.at[lax.rem(at, layers), q], near_recv.at[lax.rem(at, layers), q], slab=partner,
        )

    def far_copy(at, q):
        return remote(
            stage.at[at, q, 1 - side], landed.at[lax.rem(at, layers), side, q],
            far_send.at[at, q], far_recv.at[side, lax.rem(at, layers), q],
            tile=beyond, slab=2 * group + at // layers,
        )

    def own_term(j):
        @pl.when(j < first_own + owned)
        def _():
            at = j - first_own
            for q in range(half):
                term = jnp.concatenate(
                    conj_times((psi[j, q, 0], psi[j, q, 1]), pair(work, q)), axis=1
                )
                pick = one_hot((2 * window, window), 0, my_rows[q])
                placed = jnp.dot(
                    pick, term.astype(BF16), preferred_element_type=F32
                ).astype(BF16)
                for part in range(2):
                    rows = placed[part * window : (part + 1) * window]
                    stage[at, q, part, 0], stage[at, q, part, 1] = halves(rows, window)
                far_copy(at, q).start()

            @pl.when(at // layers != side)
            def _():
                for q in range(half):
                    near_copy(at, q).start()

    def backward(i, carried):
        j = last - i
        own_term(j)
        grads = [pair(work, q) for q in range(half)]
        inner = [conj_times(a, b) for a, b in zip(patch(j), grads)]
        moved = run(inner)
        pace = (prop[0], prop[1])
        back = run([conj(conj_times(pace, f)) for f in moved])
        for q in range(half):
            work[q, 0] = back[q][0]
            work[q, 1] = -back[q][1]
        return carried

    lax.fori_loop(0, last - first_own, backward, 0)
    own_term(first_own)

    def far_arrival(layer, of_side, q):
        return remote(
            stage.at[0, q, 0], landed.at[layer, of_side, q],
            far_send.at[0, q], far_recv.at[of_side, layer, q], slab=partner,
        )

    def near_arrival(layer, q):
        return remote(
            stage.at[0, q, 0], landed.at[layer, 3 - side, q],
            near_send.at[layer, q], near_recv.at[layer, q], slab=partner,
        )

    all_place = place[...].reshape(4 * half * window, columns)
    for layer in reversed(range(layers)):
        for q in range(half):
            landed[layer, 2 + side, q] = stage[side * layers + layer, q, side]
            near_arrival(layer, q).wait_recv()
            for of_side in range(2):
                far_arrival(layer, of_side, q).wait_recv()
        for c in range(2):
            blocks = [landed[layer, slot, q, c] for slot in range(4) for q in range(half)]
            out[c, layer] = jnp.dot(
                jnp.concatenate(blocks, axis=1), all_place, preferred_element_type=F32
            ).astype(out.dtype)

    @pl.when(side == 1)
    def _():
        for q in range(half):
            seen_copy(q).wait_send()

    for layer in range(layers):
        for q, c in pieces:
            low_copy(layer, q, c).wait_send()
            high_copy(layer, q, c).wait_send()
            give_copy(layer, q, c).wait_send()
        for q in range(half):
            near_copy((1 - side) * layers + layer, q).wait_send()
    for at in range(owned):
        for q in range(half):
            far_copy(at, q).wait_send()
        for c in range(2):
            for step in range(1, groups):
                cross_copy(step, at, c).wait_send()


def body(object_field, probe_wave, prop_phase, intensity, patch_rows, patch_cols):
    window = probe_wave.shape[1]
    layers, columns = object_field.shape[1], object_field.shape[3]
    half = intensity.shape[0] // 2
    tiles, sections = lax.axis_size("tile"), lax.axis_size("slab")
    slices = sections * layers
    groups = sections // 2
    owned = 2 * layers
    right = fourier_parts(window)
    block = (window, window)
    dma = pltpu.SemaphoreType.DMA
    return pl.pallas_call(
        functools.partial(kernel, tiles, sections),
        out_shape=jax.ShapeDtypeStruct(object_field.shape, BF16),
        in_specs=[pl.BlockSpec(memory_space=pl.ANY)] * 7,
        out_specs=pl.BlockSpec(memory_space=pltpu.VMEM),
        scratch_shapes=[
            pltpu.SMEM(patch_rows.shape, jnp.int32),
            pltpu.SMEM(patch_cols.shape, jnp.int32),
            pltpu.VMEM(object_field.shape, BF16),
            pltpu.VMEM(probe_wave.shape, BF16),
            pltpu.VMEM(prop_phase.shape, F32),
            pltpu.VMEM(intensity.shape, F32),
            pltpu.VMEM((4, half, window, columns), BF16),
            pltpu.VMEM((layers, half, 2) + block, BF16),
            pltpu.VMEM((layers, half, 2) + block, BF16),
            pltpu.VMEM((layers, half, 2) + block, BF16),
            pltpu.VMEM((owned, half, 2, 2) + block, BF16),
            pltpu.VMEM((slices, 2, half) + block, BF16),
            pltpu.VMEM((slices, half, 2) + block, F32),
            pltpu.VMEM((half, 2) + block, F32),
            pltpu.VMEM((2,) + block, F32),
            pltpu.VMEM((half,) + block, F32),
            pltpu.VMEM((owned, half, 2, 2) + block, BF16),
            pltpu.VMEM((layers, 4, half, 2) + block, BF16),
            pltpu.VMEM(right.shape, BF16),
            dma((6,)),
            dma((layers,)),
            dma((layers, half, 2)),
            dma((layers, half, 2)),
            dma((layers, half, 2)),
            dma((owned, half, 2)),
            dma((layers, half, 2)),
            dma((groups - 1, owned, 2)),
            dma((groups - 1, owned, 2)),
            dma((half,)),
            dma((half,)),
            dma((layers, half)),
            dma((layers, half)),
            dma((owned, half)),
            dma((2, layers, half)),
        ],
        compiler_params=pltpu.CompilerParams(
            collective_id=0, has_side_effects=True, vmem_limit_bytes=60 * 1024 * 1024
        ),
    )(
        patch_rows, patch_cols, object_field, probe_wave, prop_phase, intensity,
        jnp.asarray(right),
    )


def solution(mesh):
    return jax.shard_map(
        body,
        mesh=mesh,
        in_specs=(P(None, "slab", "tile", None), P(), P(), P("tile", None, None), P(), P()),
        out_specs=P(None, "slab", "tile", None),
        check_vma=False,
    )
```

time: 37.4 us -> 34.4 us (0.920)
  Pallas kernels: 35.3 us -> 32.4 us
    pallas_call x1, Pallas kernels: 35.3 us -> 32.4 us  [body(): pl.pallas_call(functools.partial(kernel, tiles, sections), out_shape=jax....]
where the time goes in v2:
time: 34.4 us; the launch traced here: 34.3 us
  Pallas kernels  32.4 us (94%)
  local copies, waits for them, and re-layouts  1.87 us (5%)
    pallas_call x1, Pallas kernels, body(): pl.pallas_call(functools.partial(kernel, tiles, sections), out_shape=jax....  32.4 us
    unnamed x1, local copies, waits for them, and re-layouts  1.87 us

profile of v2, /device:TPU:0, one launch (start us, length us, event | category | flops | bytes accessed | tf_op | source)
XLA Modules:
  0.0 34.3 jit_solution(13874110835604028618)
XLA Ops:
  0.0 32.4 %shard_map.73 = bf16[2,2,128,512]{3,2,1,0:T(8,128)(2,1)} custom-call(s32[16]{0:T(128)} %row_in.1, s32[16]{0:T(128)} %col_in.1, bf16[2,2,128,512]{3,2,1,0:T(8,128)(2,1)} %obj_in.1, bf16[2,128,128]{2,1,0:T(8,128)(2,1)} %probe_in.1, f32[128,128]{1,0:T(8,128)} %phase_in.1, f32[2,128,128]{2,1,0:T(8,128)} %measured_in.1, bf16[1280,256]{1,0:T(8,128)(2,1)} %constant.2.clone.right_in), custom_call_target="tpu_custom_call" | custom-call | tf_op jit(solution)/shard_map/pallas_call | solution.py:434
  32.4 1.9 %copy.9 = bf16[2,2,128,512]{3,2,1,0:T(8,128)(2,1)} copy(bf16[2,2,128,512]{3,2,1,0:T(8,128)(2,1)} %shard_map.73) | data formatting | bytes 1048576

commit v3 on v2

--- a/solution.py
+++ b/solution.py
@@ -96,7 +96,7 @@
     tiles, sections, row_in, col_in, obj_in, probe_in, phase_in, measured_in, right_in, out,
     row_ref, col_ref, obj, probe, phase, measured,
     place, cut_low, cut_high, cut_give, both, patches, psi, work, prop, seen, stage, landed, right,
-    load_sem, obj_sem,
+    total, load_sem, obj_sem, out_sem,
     low_send, high_send, give_send, part_recv, give_recv, cross_send, cross_recv,
     seen_send, seen_recv, near_send, near_recv, far_send, far_recv,
 ):
@@ -387,6 +387,9 @@
             near_send.at[layer, q], near_recv.at[layer, q], slab=partner,
         )
 
+    def out_copy(c, layer):
+        return pltpu.make_async_copy(total.at[c, layer], out.at[c, layer], out_sem.at[c, layer])
+
     all_place = place[...].reshape(4 * half * window, columns)
     for layer in reversed(range(layers)):
         for q in range(half):
@@ -396,9 +399,10 @@
                 far_arrival(layer, of_side, q).wait_recv()
         for c in range(2):
             blocks = [landed[layer, slot, q, c] for slot in range(4) for q in range(half)]
-            out[c, layer] = jnp.dot(
+            total[c, layer] = jnp.dot(
                 jnp.concatenate(blocks, axis=1), all_place, preferred_element_type=F32
-            ).astype(out.dtype)
+            ).astype(total.dtype)
+            out_copy(c, layer).start()
 
     @pl.when(side == 1)
     def _():
@@ -418,6 +422,9 @@
         for c in range(2):
             for step in range(1, groups):
                 cross_copy(step, at, c).wait_send()
+    for layer in range(layers):
+        for c in range(2):
+            out_copy(c, layer).wait()
 
 
 def body(object_field, probe_wave, prop_phase, intensity, patch_rows, patch_cols):
@@ -435,7 +442,7 @@
         functools.partial(kernel, tiles, sections),
         out_shape=jax.ShapeDtypeStruct(object_field.shape, BF16),
         in_specs=[pl.BlockSpec(memory_space=pl.ANY)] * 7,
-        out_specs=pl.BlockSpec(memory_space=pltpu.VMEM),
+        out_specs=pl.BlockSpec(memory_space=pl.ANY),
         scratch_shapes=[
             pltpu.SMEM(patch_rows.shape, jnp.int32),
             pltpu.SMEM(patch_cols.shape, jnp.int32),
@@ -456,8 +463,10 @@
             pltpu.VMEM((owned, half, 2, 2) + block, BF16),
             pltpu.VMEM((layers, 4, half, 2) + block, BF16),
             pltpu.VMEM(right.shape, BF16),
+            pltpu.VMEM(object_field.shape, BF16),
             dma((6,)),
             dma((layers,)),
+            dma((2, layers)),
             dma((layers, half, 2)),
             dma((layers, half, 2)),
             dma((layers, half, 2)),

time: 34.4 us -> 34.3 us (level)
  no operation moved by 1% of the time
where the time goes in v3:
time: 34.3 us; the launch traced here: 34.1 us
  Pallas kernels  32.3 us (94%)
  local copies, waits for them, and re-layouts  1.87 us (5%)
    pallas_call x1, Pallas kernels, body(): pl.pallas_call(functools.partial(kernel, tiles, sections), out_shape=jax....  32.3 us
    unnamed x1, local copies, waits for them, and re-layouts  1.87 us

profile of v3, /device:TPU:0, one launch (start us, length us, event | category | flops | bytes accessed | tf_op | source)
XLA Modules:
  0.0 34.1 jit_solution(3148251492521522508)
XLA Ops:
  0.0 32.3 %shard_map.73 = bf16[2,2,128,512]{3,2,1,0:T(8,128)(2,1)} custom-call(s32[16]{0:T(128)} %row_in.1, s32[16]{0:T(128)} %col_in.1, bf16[2,2,128,512]{3,2,1,0:T(8,128)(2,1)} %obj_in.1, bf16[2,128,128]{2,1,0:T(8,128)(2,1)} %probe_in.1, f32[128,128]{1,0:T(8,128)} %phase_in.1, f32[2,128,128]{2,1,0:T(8,128)} %measured_in.1, bf16[1280,256]{1,0:T(8,128)(2,1)} %constant.2.clone.right_in), custom_call_target="tpu_custom_call" | custom-call | tf_op jit(solution)/shard_map/pallas_call | solution.py:441
  32.3 1.9 %copy.9 = bf16[2,2,128,512]{3,2,1,0:T(8,128)(2,1)} copy(bf16[2,2,128,512]{3,2,1,0:T(8,128)(2,1)} %shard_map.73) | data formatting | bytes 1048576
